TPU v7x, 32 devices: a whole 2x2x4 slice. The times are simulated.
32 devices in a mesh: member: 8 (over z, x), domain: 4 (over y, core).
Axes of the slice: x: 2, y: 2, z: 4, core: 2. Of those that a mesh axis runs over, the one named last changes fastest.
Arguments:
- starting_tracer_fields: float32 [8, 2, 8, 64, 640], P('member', None, None, 'domain'), may hold values from -6 to 6
- surface_exchange_inputs: float32 [8, 2, 64, 640], P('member', None, 'domain'), may hold values from -4 to 4
- diffusivity: float32 [2, 8], replicated, may hold values from 0.04 to 0.2
- mixing: float32 [2, 7], replicated, may hold values from 0.02 to 0.1
- land_mask: int32 [64, 640], replicated, may hold values 0 or 1
- obs_index: int32 [4, 8, 256], P('domain'), may hold values from 0 to 1279
- obs_count: int32 [4, 8], P('domain'), may hold values from 1 to 256, as said below
- obs_value: float32 [4, 8, 256], P('domain'), may hold values from -8 to 8
- obs_error: float32 [4, 8, 256], P('domain'), may hold values from 1 to 16
Outputs:
- analysis: float32 [8, 2, 8, 64, 640], P('member', None, None, 'domain')
Inputs may be any that keep to these rules, and one draw needn't show every extreme that they name: `obs_index`: A cell of the tile's 2 x 640 surface cells, counted row by row. `obs_count`: slots below the count hold observations, the rest are unused; in every domain the last tile holds exactly 256.
All inputs are finite; a program needn't handle non-finite values.
Results may differ from a plain program's by a relative error of at most 0.0001.
Values sent between devices are 32-bit elements; how exact they have to be, the bound alone decides.
A program may use at most 64 MiB of HBM per device.

v0:
```python
import jax
import jax.numpy as jnp
from jax import lax
from jax.sharding import PartitionSpec as P

STEPS = 2


def with_halo(shard, sides, width):
    for axis, dim in sides:
        size, length = (lax.axis_size(axis), shard.shape[dim])
        up = [(i, (i + 1) % size) for i in range(size - 1)]
        down = [(j, i) for i, j in up]
        last = lax.slice_in_dim(shard, length - width, length, axis=dim)
        initial = lax.slice_in_dim(shard, 0, width, axis=dim)
        before = lax.ppermute(last, axis, up)
        after = lax.ppermute(initial, axis, down)
        shard = jnp.concatenate([before, shard, after], axis=dim)
    return shard


def stencil(padded, mask_rows, diffusivity, mixing, surface_exchange_inputs):
    middle = padded[:, :, 1:-1]
    mask_mid = mask_rows[1:-1]
    upper_row = padded[:, :, 2:]
    lower_row = padded[:, :, :-2]
    east_cell = jnp.roll(middle, -1, axis=3)
    west_cell = jnp.roll(middle, 1, axis=3)
    lateral = mask_rows[2:] * (upper_row - middle) + mask_rows[:-2] * (lower_row - middle)
    lateral = lateral + jnp.roll(mask_mid, -1, axis=1) * (east_cell - middle)
    lateral = lateral + jnp.roll(mask_mid, 1, axis=1) * (west_cell - middle)
    downward_flux = mixing[:, :, None, None] * (middle[:, 1:] - middle[:, :-1])
    empty_level = jnp.zeros_like(middle[:, :1])
    vertical = jnp.concatenate([downward_flux, empty_level], axis=1) - jnp.concatenate(
        [empty_level, downward_flux], axis=1
    )
    tendency = diffusivity[:, :, None, None] * lateral + vertical
    tendency = tendency.at[:, 0].add(surface_exchange_inputs)
    return middle + mask_mid * tendency


def partial_sums(observed, values, errors, active):
    average = jnp.mean(observed, axis=0)
    anomaly = observed - average[None, :]
    weight_obs = active / errors
    gram = jnp.dot(anomaly * weight_obs[None, :], anomaly.T, precision=lax.Precision.HIGHEST)
    pull = jnp.dot(anomaly, weight_obs * (values - average), precision=lax.Precision.HIGHEST)
    return (gram, pull)


def transform(gram, pull):
    count = gram.shape[0]
    identity = jnp.eye(count, dtype=gram.dtype)
    factor = jnp.linalg.cholesky(gram + (count - 1.0) * identity)
    inverse = jax.scipy.linalg.solve_triangular(factor, identity, lower=True)
    mean_weight = jnp.dot(
        inverse.T,
        jnp.dot(inverse, pull, precision=lax.Precision.HIGHEST),
        precision=lax.Precision.HIGHEST,
    )
    weights = mean_weight[:, None] + jnp.sqrt(count - 1.0) * inverse.T
    return weights - jnp.mean(weights, axis=0, keepdims=True) + 1.0 / count


def update(kernel, tile_block, tile_mask):
    count = tile_block.shape[0]
    updated = jnp.einsum(
        "jm,jn->mn", kernel, tile_block.reshape(count, -1), precision=lax.Precision.HIGHEST
    )
    return jnp.where(tile_mask > 0, updated.reshape(tile_block.shape), tile_block)


def shards(
    starting_tracer_fields,
    surface_exchange_inputs,
    diffusivity,
    mixing,
    land_mask,
    obs_index,
    obs_count,
    obs_value,
    obs_error,
):
    ocean_state = starting_tracer_fields[0]
    row_count = ocean_state.shape[2]
    longitudes = ocean_state.shape[3]
    subregion_offset = lax.axis_index("domain")
    sea_mask = land_mask.astype(jnp.float32)
    padded_mask = jnp.pad(sea_mask, ((1, 1), (0, 0)))
    local_mask = lax.dynamic_slice_in_dim(
        padded_mask, subregion_offset * row_count, row_count + 2, 0
    )
    for _ in range(STEPS):
        padded = with_halo(ocean_state, (("domain", 2),), 1)
        ocean_state = stencil(padded, local_mask, diffusivity, mixing, surface_exchange_inputs[0])
    stacked = ocean_state.reshape(1, -1, row_count, longitudes)
    members = lax.axis_size("member")
    tile_rows = row_count // members
    tile_index = lax.axis_index("member")
    tile_mask = lax.dynamic_slice_in_dim(local_mask[1:-1], tile_index * tile_rows, tile_rows, 0)
    slot_rank = jnp.arange(obs_index.shape[2], dtype=jnp.int32)
    tile_block = lax.all_to_all(stacked, "member", split_axis=2, concat_axis=0, tiled=True)
    surface = tile_block[:, 0].reshape(members, -1)
    obs_slots = lax.dynamic_index_in_dim(obs_index[0], tile_index, 0, keepdims=False)
    observed = surface[:, obs_slots]
    limit = lax.dynamic_index_in_dim(obs_count[0], tile_index, 0, keepdims=False)
    active = (slot_rank < limit).astype(jnp.float32)
    values = lax.dynamic_index_in_dim(obs_value[0], tile_index, 0, keepdims=False)
    errors = lax.dynamic_index_in_dim(obs_error[0], tile_index, 0, keepdims=False)
    gram, pull = partial_sums(observed, values, errors, active)
    gram, pull = lax.psum((gram, pull), "member")
    kernel = transform(gram, pull)
    updated = update(kernel, tile_block, tile_mask)
    returned = lax.all_to_all(updated, "member", split_axis=0, concat_axis=2, tiled=True)
    return returned.reshape(starting_tracer_fields.shape)


def solution(mesh):
    placed = (
        P("member", None, None, "domain", None),
        P("member", None, "domain", None),
        P(),
        P(),
        P(),
        P("domain", None, None),
        P("domain", None),
        P("domain", None, None),
        P("domain", None, None),
    )
    return jax.shard_map(
        shards,
        mesh=mesh,
        in_specs=placed,
        out_specs=P("member", None, None, "domain", None),
        check_vma=False,
    )
```

profile of v0, /device:TPU:0, one launch (start us, length us, event | category | flops | bytes accessed | tf_op | source)
XLA Modules:
  0.0 90.1 jit_solution(5743181250172521186)
XLA Ops:
  0.0 1.2 %fusion.61 = (f32[2,8,1,640]{3,2,1,0:T(1,128)S(1)}, f32[2,8,1,640]{3,2,1,0:T(1,128)S(1)}) fusion(f32[2,8,16,640]{3,2,1,0:T(8,128)} %bitcast.78), kind=kLoop, calls=%fused_computation.108 | loop fusion | bytes 163840 | tf_op jit(solution)/shard_map/slice | solution.py:15
  1.2 1.3 %collective-permute-start = (f32[2,8,1,640]{3,2,1,0:T(1,128)S(1)}, f32[2,8,1,640]{3,2,1,0:T(1,128)S(1)}, u32[]{:S(2)}, u32[]{:S(2)}) collective-permute-start(f32[2,8,1,640]{3,2,1,0:T(1,128)S(1)} %get-tuple-element.43), channel_id=1, source_target_pairs={{1,0},{2,1},{3,2},{5,4},{6,5},{7,6},{9,8},{10,9},{11,10},{13,12},{... | collective-permute-start | bytes 122888 | tf_op jit(solution)/shard_map/ppermute | solution.py:17
  2.5 3.0 %collective-permute-start.1 = (f32[2,8,1,640]{3,2,1,0:T(1,128)S(1)}, f32[2,8,1,640]{3,2,1,0:T(1,128)S(1)}, u32[]{:S(2)}, u32[]{:S(2)}) collective-permute-start(f32[2,8,1,640]{3,2,1,0:T(1,128)S(1)} %get-tuple-element.44), channel_id=1, source_target_pairs={{0,1},{1,2},{2,3},{4,5},{5,6},{6,7},{8,9},{9,10},{10,11},{12,13},{... | collective-permute-start | bytes 122888 | tf_op jit(solution)/shard_map/ppermute | solution.py:16
  5.5 1.1 %fusion.59 = (f32[2,8,16,1]{3,2,1,0:T(8,128)S(1)}, f32[2,8,16,1]{3,2,1,0:T(8,128)S(1)}) fusion(f32[2,8,16,640]{3,2,1,0:T(8,128)} %bitcast.79), kind=kLoop, calls=%fused_computation.106 | loop fusion | bytes 4096 | tf_op jit(solution)/shard_map/jit(_roll_static)/slice | solution.py:28
  6.9 0.7 copy-done.3
  7.8 0.6 copy-done.4
  8.7 0.7 copy-done.5
  9.3 0.6 fusion.15
  9.9 0.3 copy-done.2
  10.8 1.3 %collective-permute-start.2 = (f32[2,8,1,640]{3,2,1,0:T(1,128)S(1)}, f32[2,8,1,640]{3,2,1,0:T(1,128)S(1)}, u32[]{:S(2)}, u32[]{:S(2)}) collective-permute-start(f32[2,8,1,640]{3,2,1,0:T(1,128)S(1)} %get-tuple-element.37), channel_id=1, source_target_pairs={{1,0},{2,1},{3,2},{5,4},{6,5},{7,6},{9,8},{10,9},{11,10},{13,12},{... | collective-permute-start | bytes 122888 | tf_op jit(solution)/shard_map/ppermute | solution.py:17
  12.1 5.1 %collective-permute-start.3 = (f32[2,8,1,640]{3,2,1,0:T(1,128)S(1)}, f32[2,8,1,640]{3,2,1,0:T(1,128)S(1)}, u32[]{:S(2)}, u32[]{:S(2)}) collective-permute-start(f32[2,8,1,640]{3,2,1,0:T(1,128)S(1)} %get-tuple-element.38), channel_id=1, source_target_pairs={{0,1},{1,2},{2,3},{4,5},{5,6},{6,7},{8,9},{9,10},{10,11},{12,13},{... | collective-permute-start | bytes 122888 | tf_op jit(solution)/shard_map/ppermute | solution.py:16
  17.3 0.7 collective-permute-done.3
  18.1 0.6 fusion.6
  18.8 1.0 %copy.32 = f32[1,16,16,640]{3,1,0,2:T(8,128)} copy(f32[1,16,16,640]{3,2,1,0:T(8,128)S(1)} %bitcast.85) | data formatting | bytes 1310720 | tf_op jit(solution)/shard_map/reshape | solution.py:96
  19.8 5.8 %all-to-all-start = ((f32[1,16,16,640]{3,1,0,2:T(8,128)}), f32[1,16,16,640]{3,1,0,2:T(8,128)S(1)}, u32[]{:S(2)}, u32[]{:S(2)}) async-start(f32[1,16,16,640]{3,1,0,2:T(8,128)} %copy.32), calls=%async_computation | async-start | bytes 1310720 | tf_op jit(solution)/shard_map/all_to_all | solution.py:102
  25.6 0.6 constant_dynamic-slice_fusion.2
  26.2 0.7 compare_select_fusion
  26.9 0.7 constant_dynamic-slice_fusion
  27.7 15.9 %all-to-all-done = f32[1,16,16,640]{3,1,0,2:T(8,128)S(1)} async-done(((f32[1,16,16,640]{3,1,0,2:T(8,128)}), f32[1,16,16,640]{3,1,0,2:T(8,128)S(1)}, u32[]{:S(2)}, u32[]{:S(2)}) %all-to-all-start) | async-done | bytes 655392 | tf_op jit(solution)/shard_map/all_to_all | solution.py:102
  43.6 0.4 copy.55
  44.2 0.7 gather_fusion
  45.1 0.6 subtract_multiply_fusion
  46.0 0.5 fusion.27
  46.5 20.4 %all-reduce.5 = (f32[8,8]{0,1:T(8,128)S(1)}, f32[8]{0:T(128)S(1)}) all-reduce(f32[8,8]{0,1:T(8,128)S(1)} %fusion.27, f32[8]{0:T(128)S(1)} %convolution_bitcast_fusion.2), channel_id=1, replica_groups=mesh['member'=8,'domain'=4] {'member'}, use_global_device_ids=true, to_apply=%region_1.2 | all-reduce | flops 72 | bytes 576 | tf_op jit(solution)/shard_map/psum | solution.py:111
  67.0 0.7 cholesky.17
  67.9 0.6 compare_reduce_fusion
  68.6 0.6 select_select_fusion
  69.3 0.6 custom-call.7
  70.4 1.4 %convolution_select_fusion = f32[8,16,2,640]{3,0,2,1:T(8,128)S(1)} fusion(f32[1,16,8,2,640]{4,1,3,2,0:T(8,128)S(1)} %bitcast.84, pred[2,640]{1,0:T(4,128)(4,1)S(1)} %fusion.35, f32[8,8]{0,1:T(8,128)S(1)} %fusion.36, f32[8]{0:T(128)S(1)} %broadcast_multiply_fusion.1, f32[8]{0:T(128)S(1)} %convolution_bitcast_fusion), kind=kOutput, calls=%fused_computation.1 | convolution fusion | flops 15892736 | bytes 1312320 | tf_op jit(solution)/shard_map/jm,jn->mn/dot_general | solution.py:67
  71.8 0.3 copy.42
  72.2 16.9 %all_to_all.33 = f32[8,16,2,640]{3,2,1,0:T(2,128)S(1)} all-to-all(f32[8,16,2,640]{3,2,1,0:T(2,128)S(1)} %copy.42), channel_id=1, replica_groups=mesh['member'=8,'domain'=4] {'member'}, dimensions={0} | all-to-all | bytes 1310720 | tf_op jit(solution)/shard_map/all_to_all | solution.py:114
  89.1 1.0 %copy.44 = f32[1,2,8,16,640]{4,3,2,1,0:T(8,128)} copy(f32[1,2,8,16,640]{4,2,1,3,0:T(8,128)S(1)} %bitcast.86) | data formatting | bytes 1310720 | tf_op jit(solution)/shard_map/reshape | solution.py:115
  (44 shorter events, 2.9 us)
Async XLA Ops:
  0.0 25.6 %copy-start = (s32[1,8]{1,0:T(1,128)S(1)}, s32[1,8]{1,0:T(1,128)}, u32[]{:S(2)}) copy-start(s32[1,8]{1,0:T(1,128)} %param.19) | copy-start | bytes 100
  0.0 6.6 %copy-start.1 = (f32[1,2,8,16,640]{4,3,2,1,0:T(8,128)S(1)}, f32[1,2,8,16,640]{4,3,2,1,0:T(8,128)}, u32[]{:S(2)}) copy-start(f32[1,2,8,16,640]{4,3,2,1,0:T(8,128)} %param.13) | copy-start | bytes 1966084
  1.2 7.4 %collective-permute-start = (f32[2,8,1,640]{3,2,1,0:T(1,128)S(1)}, f32[2,8,1,640]{3,2,1,0:T(1,128)S(1)}, u32[]{:S(2)}, u32[]{:S(2)}) collective-permute-start(f32[2,8,1,640]{3,2,1,0:T(1,128)S(1)} %get-tuple-element.43), channel_id=1, source_target_pairs={{1,0},{2,1},{3,2},{5,4},{6,5},{7,6},{9,8},{10,9},{11,10},{13,12},{... | collective-permute-start | bytes 122888 | tf_op jit(solution)/shard_map/ppermute | solution.py:17
  2.5 6.1 %collective-permute-start.1 = (f32[2,8,1,640]{3,2,1,0:T(1,128)S(1)}, f32[2,8,1,640]{3,2,1,0:T(1,128)S(1)}, u32[]{:S(2)}, u32[]{:S(2)}) collective-permute-start(f32[2,8,1,640]{3,2,1,0:T(1,128)S(1)} %get-tuple-element.44), channel_id=1, source_target_pairs={{0,1},{1,2},{2,3},{4,5},{5,6},{6,7},{8,9},{9,10},{10,11},{12,13},{... | collective-permute-start | bytes 122888 | tf_op jit(solution)/shard_map/ppermute | solution.py:16
  6.6 0.9 %copy-start.3 = (s32[64,640]{1,0:T(8,128)S(1)}, s32[64,640]{1,0:T(8,128)}, u32[]{:S(2)}) copy-start(s32[64,640]{1,0:T(8,128)} %param.17) | copy-start | bytes 491524
  7.7 0.7 copy-start.4
  8.6 0.7 copy-start.5
  9.3 0.9 copy-start.2
  10.8 6.6 %collective-permute-start.2 = (f32[2,8,1,640]{3,2,1,0:T(1,128)S(1)}, f32[2,8,1,640]{3,2,1,0:T(1,128)S(1)}, u32[]{:S(2)}, u32[]{:S(2)}) collective-permute-start(f32[2,8,1,640]{3,2,1,0:T(1,128)S(1)} %get-tuple-element.37), channel_id=1, source_target_pairs={{1,0},{2,1},{3,2},{5,4},{6,5},{7,6},{9,8},{10,9},{11,10},{13,12},{... | collective-permute-start | bytes 122888 | tf_op jit(solution)/shard_map/ppermute | solution.py:17
  12.1 6.0 %collective-permute-start.3 = (f32[2,8,1,640]{3,2,1,0:T(1,128)S(1)}, f32[2,8,1,640]{3,2,1,0:T(1,128)S(1)}, u32[]{:S(2)}, u32[]{:S(2)}) collective-permute-start(f32[2,8,1,640]{3,2,1,0:T(1,128)S(1)} %get-tuple-element.38), channel_id=1, source_target_pairs={{0,1},{1,2},{2,3},{4,5},{5,6},{6,7},{8,9},{9,10},{10,11},{12,13},{... | collective-permute-start | bytes 122888 | tf_op jit(solution)/shard_map/ppermute | solution.py:16
  19.8 23.8 %all-to-all-start = ((f32[1,16,16,640]{3,1,0,2:T(8,128)}), f32[1,16,16,640]{3,1,0,2:T(8,128)S(1)}, u32[]{:S(2)}, u32[]{:S(2)}) async-start(f32[1,16,16,640]{3,1,0,2:T(8,128)} %copy.32), calls=%async_computation | async-start | bytes 1310720 | tf_op jit(solution)/shard_map/all_to_all | solution.py:102
where the time goes:
time: 90.7 us; the launch traced here: 90.1 us
  blocking collectives  37.3 us (41%)
  waiting for transfers between devices  16.7 us (18%)
  starting transfers between devices  16.6 us (18%)
  local copies, waits for them, and re-layouts  10.7 us (12%)
  other arithmetic  6.05 us (7%)
  matrix products  2.55 us (3%)
    psum x1, blocking collectives, shards(): gram, pull = lax.psum((gram, pull), 'member')  20.4 us
    all_to_all x1, blocking collectives, shards(): lax.all_to_all(updated, 'member', split_axis=0, concat_axis=2, tiled=True)  16.9 us
    all_to_all x1, waiting for transfers between devices, shards(): lax.all_to_all(stacked, 'member', split_axis=2, concat_axis=0, tiled=True)  15.9 us
    ppermute x2, starting transfers between devices, with_halo(): before = lax.ppermute(last, axis, up)  8.18 us
    all_to_all x1, starting transfers between devices, shards(): lax.all_to_all(stacked, 'member', split_axis=2, concat_axis=0, tiled=True)  5.81 us
    ppermute x2, starting transfers between devices, with_halo(): after = lax.ppermute(initial, axis, down)  2.58 us
    unnamed x12, local copies, waits for them, and re-layouts  2.27 us
  transfers between devices with their start and end apart: 5, of which 2 were waited for; matrix products, arithmetic and copies ran while one was open for 4% of the time, Pallas kernels for 0%

commit v1 on v0

--- a/solution.py
+++ b/solution.py
@@ -99,7 +99,12 @@
     tile_index = lax.axis_index("member")
     tile_mask = lax.dynamic_slice_in_dim(local_mask[1:-1], tile_index * tile_rows, tile_rows, 0)
     slot_rank = jnp.arange(obs_index.shape[2], dtype=jnp.int32)
-    tile_block = lax.all_to_all(stacked, "member", split_axis=2, concat_axis=0, tiled=True)
+    tile_block = jnp.concatenate(
+        lax.all_to_all(
+            jnp.stack(jnp.split(stacked, lax.axis_size("member"), axis=2)), "member", 0, 0
+        ),
+        axis=0,
+    )
     surface = tile_block[:, 0].reshape(members, -1)
     obs_slots = lax.dynamic_index_in_dim(obs_index[0], tile_index, 0, keepdims=False)
     observed = surface[:, obs_slots]

time: 90.7 us -> 94 us (1.036)
  local copies, waits for them, and re-layouts: 10.7 us -> 14.3 us
    unnamed x12 -> x22, local copies, waits for them, and re-layouts: 2.27 us -> 7.77 us
    another operation x0 -> x2, local copies, waits for them, and re-layouts: none -> 1.21 us  [the longest x1 0.67 us: shards(): jnp.stack(jnp.split(stacked, lax.axis_size('member'), axis=2))]
    slice x2, local copies, waits for them, and re-layouts: 1.26 us -> 0.12 us  [with_halo(): initial = lax.slice_in_dim(shard, 0, width, axis=dim)]
    reshape x1 -> x0, local copies, waits for them, and re-layouts: 1.04 us -> none  [shards(): stacked = ocean_state.reshape(1, -1, row_count, longitudes)]
    slice x4, local copies, waits for them, and re-layouts: 1.64 us -> 0.67 us  [stencil(): west_cell = jnp.roll(middle, 1, axis=3)]
  transfers between devices with their start and end apart: 5 -> 5, of which waited for: 2 -> 2; matrix products, arithmetic and copies ran while one was open for 4% -> 3% of each run, Pallas kernels for 0% -> 0%
where the time goes in v1:
time: 94 us; the launch traced here: 93.5 us
  blocking collectives  37.3 us (40%)
  waiting for transfers between devices  16.7 us (18%)
  starting transfers between devices  16.6 us (18%)
  local copies, waits for them, and re-layouts  14.3 us (15%)
  other arithmetic  6.08 us (6%)
  matrix products  2.29 us (2%)
    psum x1, blocking collectives, shards(): gram, pull = lax.psum((gram, pull), 'member')  20.4 us
    all_to_all x1, blocking collectives, shards(): lax.all_to_all(updated, 'member', split_axis=0, concat_axis=2, tiled=True)  16.9 us
    all_to_all x1, waiting for transfers between devices, shards(): lax.all_to_all(jnp.stack(jnp.split(stacked, lax.axis_size('member'), axis...  15.9 us
    ppermute x2, starting transfers between devices, with_halo(): before = lax.ppermute(last, axis, up)  8.18 us
    unnamed x22, local copies, waits for them, and re-layouts  7.77 us
    all_to_all x1, starting transfers between devices, shards(): lax.all_to_all(jnp.stack(jnp.split(stacked, lax.axis_size('member'), axis...  5.81 us
    ppermute x2, starting transfers between devices, with_halo(): after = lax.ppermute(initial, axis, down)  2.58 us
  transfers between devices with their start and end apart: 5, of which 2 were waited for; matrix products, arithmetic and copies ran while one was open for 3% of the time, Pallas kernels for 0%

profile of v1, /device:TPU:0, one launch (start us, length us, event | category | flops | bytes accessed | tf_op | source)
XLA Modules:
  0.0 93.5 jit_solution(16959842292837205797)
XLA Ops:
  0.0 1.1 %copy.61 = f32[1,2,8,16,640]{4,3,1,2,0:T(8,128)S(1)} copy(f32[1,2,8,16,640]{4,3,2,1,0:T(8,128)} %param.13) | data formatting | bytes 1310720 | tf_op args[0]
  1.2 1.3 %collective-permute-start = (f32[2,8,1,640]{3,2,0,1:T(1,128)S(1)}, f32[2,8,1,640]{3,2,0,1:T(1,128)S(1)}, u32[]{:S(2)}, u32[]{:S(2)}) collective-permute-start(f32[2,8,1,640]{3,2,0,1:T(1,128)S(1)} %get-tuple-element.43), channel_id=1, source_target_pairs={{1,0},{2,1},{3,2},{5,4},{6,5},{7,6},{9,8},{10,9},{11,10},{13,12},{... | collective-permute-start | bytes 122888 | tf_op jit(solution)/shard_map/ppermute | solution.py:17
  2.5 3.0 %collective-permute-start.1 = (f32[2,8,1,640]{3,2,0,1:T(1,128)S(1)}, f32[2,8,1,640]{3,2,0,1:T(1,128)S(1)}, u32[]{:S(2)}, u32[]{:S(2)}) collective-permute-start(f32[2,8,1,640]{3,2,0,1:T(1,128)S(1)} %get-tuple-element.44), channel_id=1, source_target_pairs={{0,1},{1,2},{2,3},{4,5},{5,6},{6,7},{8,9},{9,10},{10,11},{12,13},{... | collective-permute-start | bytes 122888 | tf_op jit(solution)/shard_map/ppermute | solution.py:16
  5.9 0.7 copy-done.4
  7.8 0.6 fusion.15
  9.5 1.3 %collective-permute-start.2 = (f32[2,8,1,640]{3,2,0,1:T(1,128)S(1)}, f32[2,8,1,640]{3,2,0,1:T(1,128)S(1)}, u32[]{:S(2)}, u32[]{:S(2)}) collective-permute-start(f32[2,8,1,640]{3,2,0,1:T(1,128)S(1)} %get-tuple-element.37), channel_id=1, source_target_pairs={{1,0},{2,1},{3,2},{5,4},{6,5},{7,6},{9,8},{10,9},{11,10},{13,12},{... | collective-permute-start | bytes 122888 | tf_op jit(solution)/shard_map/ppermute | solution.py:17
  10.8 5.1 %collective-permute-start.3 = (f32[2,8,1,640]{3,2,0,1:T(1,128)S(1)}, f32[2,8,1,640]{3,2,0,1:T(1,128)S(1)}, u32[]{:S(2)}, u32[]{:S(2)}) collective-permute-start(f32[2,8,1,640]{3,2,0,1:T(1,128)S(1)} %get-tuple-element.38), channel_id=1, source_target_pairs={{0,1},{1,2},{2,3},{4,5},{5,6},{6,7},{8,9},{9,10},{10,11},{12,13},{... | collective-permute-start | bytes 122888 | tf_op jit(solution)/shard_map/ppermute | solution.py:16
  16.0 0.7 collective-permute-done.3
  16.8 0.6 fusion.6
  17.6 0.7 fusion.35
  18.2 0.7 fusion.34
  18.9 0.7 fusion.33
  19.6 0.7 fusion.32
  20.2 0.7 fusion.31
  20.9 0.7 fusion.30
  21.6 0.7 fusion.29
  22.2 0.7 fusion.28
  22.9 5.8 %all-to-all-start = ((f32[8,1,16,2,640]{4,3,2,1,0:T(2,128)}), f32[8,1,16,2,640]{4,3,2,1,0:T(2,128)S(1)}, u32[]{:S(2)}, u32[]{:S(2)}) async-start(f32[8,1,16,2,640]{4,3,2,1,0:T(2,128)} %fusion.28), calls=%async_computation | async-start | bytes 1310720 | tf_op jit(solution)/shard_map/all_to_all | solution.py:103
  28.7 0.6 constant_dynamic-slice_fusion.2
  29.3 0.7 compare_select_fusion
  30.0 0.7 constant_dynamic-slice_fusion
  30.8 15.9 %all-to-all-done = f32[8,1,16,2,640]{4,3,2,1,0:T(2,128)S(1)} async-done(((f32[8,1,16,2,640]{4,3,2,1,0:T(2,128)}), f32[8,1,16,2,640]{4,3,2,1,0:T(2,128)S(1)}, u32[]{:S(2)}, u32[]{:S(2)}) %all-to-all-start) | async-done | bytes 655392 | tf_op jit(solution)/shard_map/all_to_all | solution.py:103
  47.3 0.7 gather_fusion
  48.2 0.6 subtract_multiply_fusion
  49.6 20.4 %all-reduce.5 = (f32[8,8]{0,1:T(8,128)S(1)}, f32[8]{0:T(128)S(1)}) all-reduce(f32[8,8]{0,1:T(8,128)S(1)} %fusion.25, f32[8]{0:T(128)S(1)} %convolution_bitcast_fusion.2), channel_id=1, replica_groups=mesh['member'=8,'domain'=4] {'member'}, use_global_device_ids=true, to_apply=%region_1.2 | all-reduce | flops 72 | bytes 576 | tf_op jit(solution)/shard_map/psum | solution.py:116
  70.1 0.7 cholesky.17
  71.0 0.6 compare_reduce_fusion
  71.7 0.6 select_select_fusion
  72.4 0.6 custom-call.7
  74.1 1.1 %convolution_select_fusion = f32[8,16,2,640]{3,0,2,1:T(8,128)S(1)} fusion(f32[16,2,640,8]{2,3,1,0:T(8,128)S(1)} %bitcast.119, pred[2,640]{1,0:T(4,128)(4,1)S(1)} %fusion.41, f32[8,8]{0,1:T(8,128)S(1)} %fusion.42, f32[8]{0:T(128)S(1)} %broadcast_multiply_fusion.1, f32[8]{0:T(128)S(1)} %convolution_bitcast_fusion, f32[8,1,16,2,640]{4,3,2,1,0:T(2,128)S(1)} %all-to-all-done), kind=kOutput, calls=%fused_computation.1 | convolution fusion | flops 15892736 | bytes 1967680 | tf_op jit(solution)/shard_map/jm,jn->mn/dot_general | solution.py:67
  75.6 16.9 %all_to_all.20 = f32[8,16,2,640]{3,2,1,0:T(2,128)S(1)} all-to-all(f32[8,16,2,640]{3,2,1,0:T(2,128)S(1)} %copy.48), channel_id=1, replica_groups=mesh['member'=8,'domain'=4] {'member'}, dimensions={0} | all-to-all | bytes 1310720 | tf_op jit(solution)/shard_map/all_to_all | solution.py:119
  92.5 1.0 %copy.50 = f32[1,2,8,16,640]{4,3,2,1,0:T(8,128)} copy(f32[1,2,8,16,640]{4,2,1,3,0:T(8,128)S(1)} %bitcast.120) | data formatting | bytes 1310720 | tf_op jit(solution)/shard_map/reshape | solution.py:120
  (56 shorter events, 6.1 us)
Async XLA Ops:
  0.0 28.7 %copy-start = (s32[1,8]{1,0:T(1,128)S(1)}, s32[1,8]{1,0:T(1,128)}, u32[]{:S(2)}) copy-start(s32[1,8]{1,0:T(1,128)} %param.19) | copy-start | bytes 100
  1.2 6.6 %collective-permute-start = (f32[2,8,1,640]{3,2,0,1:T(1,128)S(1)}, f32[2,8,1,640]{3,2,0,1:T(1,128)S(1)}, u32[]{:S(2)}, u32[]{:S(2)}) collective-permute-start(f32[2,8,1,640]{3,2,0,1:T(1,128)S(1)} %get-tuple-element.43), channel_id=1, source_target_pairs={{1,0},{2,1},{3,2},{5,4},{6,5},{7,6},{9,8},{10,9},{11,10},{13,12},{... | collective-permute-start | bytes 122888 | tf_op jit(solution)/shard_map/ppermute | solution.py:17
  2.5 5.3 %collective-permute-start.1 = (f32[2,8,1,640]{3,2,0,1:T(1,128)S(1)}, f32[2,8,1,640]{3,2,0,1:T(1,128)S(1)}, u32[]{:S(2)}, u32[]{:S(2)}) collective-permute-start(f32[2,8,1,640]{3,2,0,1:T(1,128)S(1)} %get-tuple-element.44), channel_id=1, source_target_pairs={{0,1},{1,2},{2,3},{4,5},{5,6},{6,7},{8,9},{9,10},{10,11},{12,13},{... | collective-permute-start | bytes 122888 | tf_op jit(solution)/shard_map/ppermute | solution.py:16
  5.7 1.0 %copy-start.3 = (s32[64,640]{1,0:T(8,128)S(1)}, s32[64,640]{1,0:T(8,128)}, u32[]{:S(2)}) copy-start(s32[64,640]{1,0:T(8,128)} %param.17) | copy-start | bytes 491524
  5.9 0.7 copy-start.4
  7.1 0.7 copy-start.5
  7.8 0.9 copy-start.2
  7.8 1.1 %copy-start.1 = (f32[1,2,8,16,640]{4,3,2,1,0:T(8,128)S(1)}, f32[1,2,8,16,640]{4,3,2,1,0:T(8,128)}, u32[]{:S(2)}) copy-start(f32[1,2,8,16,640]{4,3,2,1,0:T(8,128)} %param.13) | copy-start | bytes 1966084
  9.5 6.6 %collective-permute-start.2 = (f32[2,8,1,640]{3,2,0,1:T(1,128)S(1)}, f32[2,8,1,640]{3,2,0,1:T(1,128)S(1)}, u32[]{:S(2)}, u32[]{:S(2)}) collective-permute-start(f32[2,8,1,640]{3,2,0,1:T(1,128)S(1)} %get-tuple-element.37), channel_id=1, source_target_pairs={{1,0},{2,1},{3,2},{5,4},{6,5},{7,6},{9,8},{10,9},{11,10},{13,12},{... | collective-permute-start | bytes 122888 | tf_op jit(solution)/shard_map/ppermute | solution.py:17
  10.8 6.0 %collective-permute-start.3 = (f32[2,8,1,640]{3,2,0,1:T(1,128)S(1)}, f32[2,8,1,640]{3,2,0,1:T(1,128)S(1)}, u32[]{:S(2)}, u32[]{:S(2)}) collective-permute-start(f32[2,8,1,640]{3,2,0,1:T(1,128)S(1)} %get-tuple-element.38), channel_id=1, source_target_pairs={{0,1},{1,2},{2,3},{4,5},{5,6},{6,7},{8,9},{9,10},{10,11},{12,13},{... | collective-permute-start | bytes 122888 | tf_op jit(solution)/shard_map/ppermute | solution.py:16
  22.9 23.8 %all-to-all-start = ((f32[8,1,16,2,640]{4,3,2,1,0:T(2,128)}), f32[8,1,16,2,640]{4,3,2,1,0:T(2,128)S(1)}, u32[]{:S(2)}, u32[]{:S(2)}) async-start(f32[8,1,16,2,640]{4,3,2,1,0:T(2,128)} %fusion.28), calls=%async_computation | async-start | bytes 1310720 | tf_op jit(solution)/shard_map/all_to_all | solution.py:103
